TPU v7x, 32 devices: a whole 2x2x4 slice. The times are simulated.
32 devices in a mesh: fsdp: 8 (over y, x, core), seq: 4 (over z).
Axes of the slice: x: 2, y: 2, z: 4, core: 2. Of those that a mesh axis runs over, the one named last changes fastest.
Arguments:
- tokens: bfloat16 [12288, 1024], P(('fsdp', 'seq')), may hold values from -6 to 6
- segment_ids: int32 [12288], P(('fsdp', 'seq')), may hold values from -1 to 1, as said below
- ln1_gain: bfloat16 [1024], P('fsdp'), may hold values from 0.099609375 to 1.8984375
- ln1_bias: bfloat16 [1024], P('fsdp'), may hold values from -3 to 3
- w_qkv: bfloat16 [1024, 3072], P('fsdp'), may hold values from -0.1875 to 0.1875
- q_bias: bfloat16 [1024], P('fsdp'), may hold values from -3 to 3
- v_bias: bfloat16 [1024], P('fsdp'), may hold values from -3 to 3
- w_out: bfloat16 [1024, 1024], P('fsdp'), may hold values from -0.75 to 0.75
- out_bias: bfloat16 [1024], P('fsdp'), may hold values from -3 to 3
- ln2_gain: bfloat16 [1024], P('fsdp'), may hold values from 0.099609375 to 1.8984375
- ln2_bias: bfloat16 [1024], P('fsdp'), may hold values from -3 to 3
- w_fc1: bfloat16 [1024, 4096], P('fsdp'), may hold values from -0.1875 to 0.1875
- fc1_bias: bfloat16 [4096], P('fsdp'), may hold values from -3 to 3
- w_fc2: bfloat16 [4096, 1024], P('fsdp'), may hold values from -0.09375 to 0.09375
- fc2_bias: bfloat16 [1024], P('fsdp'), may hold values from -3 to 3
- cotangent: bfloat16 [12288, 1024], P(('fsdp', 'seq')), may hold values from -6 to 6
Outputs:
- layer_output: bfloat16 [12288, 1024], P(('fsdp', 'seq'))
- tokens_grad: float32 [12288, 1024], P(('fsdp', 'seq'))
- ln1_gain_grad: float32 [1024], P(('fsdp', 'seq'))
- ln1_bias_grad: float32 [1024], P(('fsdp', 'seq'))
- w_qkv_grad: float32 [1024, 3072], P('fsdp', 'seq')
- q_bias_grad: float32 [1024], P(('fsdp', 'seq'))
- v_bias_grad: float32 [1024], P(('fsdp', 'seq'))
- w_out_grad: float32 [1024, 1024], P('fsdp', 'seq')
- out_bias_grad: float32 [1024], P(('fsdp', 'seq'))
- ln2_gain_grad: float32 [1024], P(('fsdp', 'seq'))
- ln2_bias_grad: float32 [1024], P(('fsdp', 'seq'))
- w_fc1_grad: float32 [1024, 4096], P('fsdp', 'seq')
- fc1_bias_grad: float32 [4096], P(('fsdp', 'seq'))
- w_fc2_grad: float32 [4096, 1024], P('fsdp', 'seq')
- fc2_bias_grad: float32 [1024], P(('fsdp', 'seq'))
Inputs may be any that keep to these rules, and one draw needn't show every extreme that they name: `segment_ids`: each span of 1536 slots (one index of fsdp) holds whole images of 577 slots from its first slot on, numbered 0, 1, 2, ... within the span, then padding slots marked -1; every span holds at least half of 2 images and some span holds 2.
All inputs are finite; a program needn't handle non-finite values.
Results may differ from a plain program's by a relative error of at most 0.019.
Values may be sent and summed in bfloat16 or wider, within the bound.
No kernel may reach another device: no remote copies, remote signals or barrier semaphores. Data moves between devices by JAX's collectives and lax.ppermute only.
A program may use at most 192 MiB of HBM per device.

v0:
```python
from functools import partial
import jax
import jax.numpy as jnp
from jax import lax
from jax.sharding import PartitionSpec as P

HD = 64
LEN = 577
norm_eps = 1e-06
masked_score = -1000000000.0


def normalize(values, gain, shift):
    row_mean = jnp.mean(values, axis=-1, keepdims=True)
    centered = values - row_mean
    variance = jnp.mean(centered * centered, axis=-1, keepdims=True)
    return centered * lax.rsqrt(variance + norm_eps) * gain + shift


def contract_rows(left, right):
    return lax.dot_general(
        left, right, (((0,), (0,)), ((), ())), preferred_element_type=jnp.float32
    )


def times_transposed(left, right):
    return lax.dot_general(
        left, right, (((1,), (1,)), ((), ())), preferred_element_type=jnp.float32
    )


def column_sum(values):
    return jnp.sum(values, axis=0, dtype=jnp.float32)


def shards_per_block(row_count, seq_count):
    for factor in range(1, seq_count + 1):
        if seq_count % factor == 0 and (row_count * factor >= 512 or factor == seq_count):
            return factor
    return seq_count


def add_window(total, delta, start):
    current = lax.dynamic_slice_in_dim(total, start, delta.shape[0], 0)
    return lax.dynamic_update_slice_in_dim(total, current + delta, start, 0)


def shards(
    tokens,
    segment_ids,
    ln1_gain,
    ln1_bias,
    w_qkv,
    q_bias,
    v_bias,
    w_out,
    out_bias,
    ln2_gain,
    ln2_bias,
    w_fc1,
    fc1_bias,
    w_fc2,
    fc2_bias,
    cotangent,
):
    row_count = tokens.shape[0]
    feature_width = tokens.shape[1]
    seq_count = lax.axis_size("seq")
    span_rows = row_count * seq_count
    local_heads = feature_width // seq_count // HD
    block_rows = row_count * shards_per_block(row_count, seq_count)
    block_count = span_rows // block_rows
    margin = LEN - 1
    window = block_rows + 2 * margin
    offsets = jnp.arange(block_count, dtype=jnp.int32) * block_rows
    scale = HD ** (-0.5)
    as_float = jnp.float32

    def weight_grad(left, right):
        return contract_rows(left, right)

    attn_set = (
        lax.all_gather(ln1_gain, "fsdp", axis=0, tiled=True),
        lax.all_gather(ln1_bias, "fsdp", axis=0, tiled=True),
        lax.all_gather(w_qkv, "fsdp", axis=0, tiled=True),
        lax.all_gather(q_bias, "fsdp", axis=0, tiled=True),
        lax.all_gather(v_bias, "fsdp", axis=0, tiled=True),
        lax.all_gather(w_out, "fsdp", axis=0, tiled=True),
        lax.all_gather(out_bias, "fsdp", axis=0, tiled=True),
    )
    span_labels = lax.all_gather(segment_ids, "seq", axis=0, tiled=True)
    inputs = tokens.astype(as_float)
    gain_one = attn_set[0].astype(as_float)
    shift_one = attn_set[1].astype(as_float)
    first_norm = normalize(inputs, gain_one, shift_one).astype(jnp.bfloat16)
    projected = jnp.dot(first_norm, attn_set[2], preferred_element_type=as_float)
    bias_all = jnp.concatenate(
        [
            attn_set[3].astype(as_float),
            jnp.zeros((feature_width,), as_float),
            attn_set[4].astype(as_float),
        ]
    )
    packed = (projected + bias_all).astype(jnp.bfloat16).reshape(row_count, 3, feature_width)
    head_rows = lax.all_to_all(packed, "seq", split_axis=2, concat_axis=0, tiled=True)
    query_heads = head_rows[:, 0, :].reshape(span_rows, local_heads, HD)
    key_heads = head_rows[:, 1, :].reshape(span_rows, local_heads, HD)
    value_heads = head_rows[:, 2, :].reshape(span_rows, local_heads, HD)
    key_padded = jnp.pad(key_heads, ((margin, margin), (0, 0), (0, 0)))
    value_padded = jnp.pad(value_heads, ((margin, margin), (0, 0), (0, 0)))
    label_padded = jnp.pad(span_labels, (margin, margin), constant_values=-2)

    def block_scores(offset):
        query_block = lax.dynamic_slice_in_dim(query_heads, offset, block_rows, 0)
        label_block = lax.dynamic_slice_in_dim(span_labels, offset, block_rows, 0)
        key_window = lax.dynamic_slice_in_dim(key_padded, offset, window, 0)
        value_window = lax.dynamic_slice_in_dim(value_padded, offset, window, 0)
        label_window = lax.dynamic_slice_in_dim(label_padded, offset, window, 0)
        scaled = (
            jnp.einsum("qhd,khd->hqk", query_block, key_window, preferred_element_type=as_float)
            * scale
        )
        same_image = label_block[:, None] == label_window[None, :]
        return (
            query_block,
            key_window,
            value_window,
            jnp.where(same_image[None], scaled, masked_score),
        )

    def block_forward(offset):
        unused_query, unused_key, value_window, scores = block_scores(offset)
        row_peak = jnp.max(scores, axis=-1, keepdims=True)
        lifted = jnp.exp(scores - row_peak)
        row_total = jnp.sum(lifted, axis=-1, keepdims=True)
        attn_probs = (lifted / row_total).astype(jnp.bfloat16)
        block_out = jnp.einsum(
            "hqk,khd->qhd", attn_probs, value_window, preferred_element_type=as_float
        ).astype(jnp.bfloat16)
        return (block_out, (row_peak + jnp.log(row_total))[..., 0])

    head_out, log_totals = lax.map(block_forward, offsets)
    head_flat = head_out.reshape(span_rows, local_heads * HD)
    attended = lax.all_to_all(head_flat, "seq", split_axis=0, concat_axis=1, tiled=True)
    mixed = jnp.dot(attended, attn_set[5], preferred_element_type=as_float) + attn_set[6].astype(
        as_float
    )
    middle = inputs + mixed
    mlp_set = (
        lax.all_gather(ln2_gain, "fsdp", axis=0, tiled=True),
        lax.all_gather(ln2_bias, "fsdp", axis=0, tiled=True),
        lax.all_gather(w_fc1, "fsdp", axis=0, tiled=True),
        lax.all_gather(fc1_bias, "fsdp", axis=0, tiled=True),
        lax.all_gather(w_fc2, "fsdp", axis=0, tiled=True),
        lax.all_gather(fc2_bias, "fsdp", axis=0, tiled=True),
    )
    gain_two = mlp_set[0].astype(as_float)
    shift_two = mlp_set[1].astype(as_float)
    second_norm = normalize(middle, gain_two, shift_two).astype(jnp.bfloat16)
    hidden = jnp.dot(second_norm, mlp_set[2], preferred_element_type=as_float) + mlp_set[3].astype(
        as_float
    )
    activated = jax.nn.gelu(hidden, approximate=False).astype(jnp.bfloat16)
    branch = jnp.dot(activated, mlp_set[4], preferred_element_type=as_float) + mlp_set[5].astype(
        as_float
    )
    valid = (segment_ids >= 0).astype(as_float)[:, None]
    layer_output = (valid * (middle + branch)).astype(jnp.bfloat16)
    grad_out = valid * cotangent.astype(as_float)
    grad_branch = grad_out.astype(jnp.bfloat16)
    fc2_bias_part = column_sum(grad_branch)
    w_fc2_part = weight_grad(activated, grad_branch)
    grad_act = times_transposed(grad_branch, mlp_set[4])
    unused_hidden, gelu_back = jax.vjp(partial(jax.nn.gelu, approximate=False), hidden)
    grad_hidden = gelu_back(grad_act)[0].astype(jnp.bfloat16)
    fc1_bias_part = column_sum(grad_hidden)
    w_fc1_part = weight_grad(second_norm, grad_hidden)
    grad_norm_two = times_transposed(grad_hidden, mlp_set[2])
    unused_two, norm_two_back = jax.vjp(
        normalize, middle, mlp_set[0].astype(as_float), mlp_set[1].astype(as_float)
    )
    grad_mid_norm, ln2_gain_part, ln2_bias_part = norm_two_back(grad_norm_two)
    grad_middle = grad_out + grad_mid_norm
    grad_mixed = grad_middle.astype(jnp.bfloat16)
    out_bias_part = column_sum(grad_mixed)
    w_out_part = weight_grad(attended, grad_mixed)
    grad_attended = times_transposed(grad_mixed, attn_set[5]).astype(jnp.bfloat16)
    grad_heads = lax.all_to_all(
        grad_attended, "seq", split_axis=1, concat_axis=0, tiled=True
    ).reshape(span_rows, local_heads, HD)

    def block_backward(running, inputs_block):
        key_total, value_total = running
        offset, log_block = inputs_block
        query_block, key_window, value_window, scores = block_scores(offset)
        grad_block = lax.dynamic_slice_in_dim(grad_heads, offset, block_rows, 0)
        probs_full = jnp.exp(scores - log_block[..., None])
        attn_probs = probs_full.astype(jnp.bfloat16)
        value_delta = jnp.einsum(
            "hqk,qhd->khd", attn_probs, grad_block, preferred_element_type=as_float
        )
        grad_probs = jnp.einsum(
            "qhd,khd->hqk", grad_block, value_window, preferred_element_type=as_float
        )
        row_inner = jnp.sum(grad_probs * probs_full, axis=-1, keepdims=True)
        grad_scores = (probs_full * (grad_probs - row_inner)).astype(jnp.bfloat16)
        grad_query = (
            jnp.einsum("hqk,khd->qhd", grad_scores, key_window, preferred_element_type=as_float)
            * scale
        )
        key_delta = (
            jnp.einsum("hqk,qhd->khd", grad_scores, query_block, preferred_element_type=as_float)
            * scale
        )
        return (
            (
                add_window(key_total, key_delta, offset),
                add_window(value_total, value_delta, offset),
            ),
            grad_query,
        )

    zero_heads = jnp.zeros((span_rows + 2 * margin, local_heads, HD), as_float)
    (key_padded_grad, value_padded_grad), query_grad = lax.scan(
        block_backward, (zero_heads, zero_heads), (offsets, log_totals)
    )
    key_grad = key_padded_grad[margin : margin + span_rows]
    value_grad = value_padded_grad[margin : margin + span_rows]
    head_grads = jnp.concatenate(
        [
            query_grad.reshape(span_rows, 1, local_heads * HD),
            key_grad.reshape(span_rows, 1, local_heads * HD),
            value_grad.reshape(span_rows, 1, local_heads * HD),
        ],
        axis=1,
    ).astype(jnp.bfloat16)
    token_grads = lax.all_to_all(
        head_grads, "seq", split_axis=0, concat_axis=2, tiled=True
    ).reshape(row_count, 3 * feature_width)
    q_bias_part = column_sum(token_grads[:, :feature_width])
    v_bias_part = column_sum(token_grads[:, 2 * feature_width :])
    w_qkv_part = weight_grad(first_norm, token_grads)
    grad_norm_one = times_transposed(token_grads, attn_set[2])
    unused_one, norm_one_back = jax.vjp(
        normalize, inputs, attn_set[0].astype(as_float), attn_set[1].astype(as_float)
    )
    grad_input_norm, ln1_gain_part, ln1_bias_part = norm_one_back(grad_norm_one)
    tokens_grad = grad_middle + grad_input_norm
    partial_sums = (
        lax.psum_scatter(
            ln1_gain_part.astype(jnp.bfloat16), "fsdp", scatter_dimension=0, tiled=True
        ).astype(jnp.float32),
        lax.psum_scatter(
            ln1_bias_part.astype(jnp.bfloat16), "fsdp", scatter_dimension=0, tiled=True
        ).astype(jnp.float32),
        lax.psum_scatter(
            w_qkv_part.astype(jnp.bfloat16), "fsdp", scatter_dimension=0, tiled=True
        ).astype(jnp.float32),
        lax.psum_scatter(
            q_bias_part.astype(jnp.bfloat16), "fsdp", scatter_dimension=0, tiled=True
        ).astype(jnp.float32),
        lax.psum_scatter(
            v_bias_part.astype(jnp.bfloat16), "fsdp", scatter_dimension=0, tiled=True
        ).astype(jnp.float32),
        lax.psum_scatter(
            w_out_part.astype(jnp.bfloat16), "fsdp", scatter_dimension=0, tiled=True
        ).astype(jnp.float32),
        lax.psum_scatter(
            out_bias_part.astype(jnp.bfloat16), "fsdp", scatter_dimension=0, tiled=True
        ).astype(jnp.float32),
        lax.psum_scatter(
            ln2_gain_part.astype(jnp.bfloat16), "fsdp", scatter_dimension=0, tiled=True
        ).astype(jnp.float32),
        lax.psum_scatter(
            ln2_bias_part.astype(jnp.bfloat16), "fsdp", scatter_dimension=0, tiled=True
        ).astype(jnp.float32),
        lax.psum_scatter(
            w_fc1_part.astype(jnp.bfloat16), "fsdp", scatter_dimension=0, tiled=True
        ).astype(jnp.float32),
        lax.psum_scatter(
            fc1_bias_part.astype(jnp.bfloat16), "fsdp", scatter_dimension=0, tiled=True
        ).astype(jnp.float32),
        lax.psum_scatter(
            w_fc2_part.astype(jnp.bfloat16), "fsdp", scatter_dimension=0, tiled=True
        ).astype(jnp.float32),
        lax.psum_scatter(
            fc2_bias_part.astype(jnp.bfloat16), "fsdp", scatter_dimension=0, tiled=True
        ).astype(jnp.float32),
    )
    summed = (
        lax.psum_scatter(
            partial_sums[0].astype(jnp.bfloat16), "seq", scatter_dimension=0, tiled=True
        ).astype(jnp.float32),
        lax.psum_scatter(
            partial_sums[1].astype(jnp.bfloat16), "seq", scatter_dimension=0, tiled=True
        ).astype(jnp.float32),
        lax.psum_scatter(
            partial_sums[2].astype(jnp.bfloat16), "seq", scatter_dimension=1, tiled=True
        ).astype(jnp.float32),
        lax.psum_scatter(
            partial_sums[3].astype(jnp.bfloat16), "seq", scatter_dimension=0, tiled=True
        ).astype(jnp.float32),
        lax.psum_scatter(
            partial_sums[4].astype(jnp.bfloat16), "seq", scatter_dimension=0, tiled=True
        ).astype(jnp.float32),
        lax.psum_scatter(
            partial_sums[5].astype(jnp.bfloat16), "seq", scatter_dimension=1, tiled=True
        ).astype(jnp.float32),
        lax.psum_scatter(
            partial_sums[6].astype(jnp.bfloat16), "seq", scatter_dimension=0, tiled=True
        ).astype(jnp.float32),
        lax.psum_scatter(
            partial_sums[7].astype(jnp.bfloat16), "seq", scatter_dimension=0, tiled=True
        ).astype(jnp.float32),
        lax.psum_scatter(
            partial_sums[8].astype(jnp.bfloat16), "seq", scatter_dimension=0, tiled=True
        ).astype(jnp.float32),
        lax.psum_scatter(
            partial_sums[9].astype(jnp.bfloat16), "seq", scatter_dimension=1, tiled=True
        ).astype(jnp.float32),
        lax.psum_scatter(
            partial_sums[10].astype(jnp.bfloat16), "seq", scatter_dimension=0, tiled=True
        ).astype(jnp.float32),
        lax.psum_scatter(
            partial_sums[11].astype(jnp.bfloat16), "seq", scatter_dimension=1, tiled=True
        ).astype(jnp.float32),
        lax.psum_scatter(
            partial_sums[12].astype(jnp.bfloat16), "seq", scatter_dimension=0, tiled=True
        ).astype(jnp.float32),
    )
    return (
        layer_output,
        tokens_grad,
        summed[0],
        summed[1],
        summed[2],
        summed[3],
        summed[4],
        summed[5],
        summed[6],
        summed[7],
        summed[8],
        summed[9],
        summed[10],
        summed[11],
        summed[12],
    )


def solution(mesh):
    return jax.shard_map(
        shards,
        mesh=mesh,
        in_specs=(
            P(("fsdp", "seq"), None),
            P(("fsdp", "seq")),
            P("fsdp"),
            P("fsdp"),
            P("fsdp", None),
            P("fsdp"),
            P("fsdp"),
            P("fsdp", None),
            P("fsdp"),
            P("fsdp"),
            P("fsdp"),
            P("fsdp", None),
            P("fsdp"),
            P("fsdp", None),
            P("fsdp"),
            P(("fsdp", "seq"), None),
        ),
        out_specs=(
            P(("fsdp", "seq"), None),
            P(("fsdp", "seq"), None),
            P(("fsdp", "seq")),
            P(("fsdp", "seq")),
            P("fsdp", "seq"),
            P(("fsdp", "seq")),
            P(("fsdp", "seq")),
            P("fsdp", "seq"),
            P(("fsdp", "seq")),
            P(("fsdp", "seq")),
            P(("fsdp", "seq")),
            P("fsdp", "seq"),
            P(("fsdp", "seq")),
            P("fsdp", "seq"),
            P(("fsdp", "seq")),
        ),
        check_vma=False,
    )
```

profile of v0, /device:TPU:0, one launch (start us, length us, event | category | flops | bytes accessed | tf_op | source)
XLA Modules:
  0.0 857.5 jit_solution(11295137797014356997)
XLA Ops:
  9.4 10.3 %all-gather.3 = bf16[8,1,128]{2,1,0:T(2,128)(2,1)S(1)} all-gather(bf16[1,1,128]{2,1,0:T(2,128)(2,1)} %bitcast.145), channel_id=1, replica_groups=mesh['fsdp'=8,'seq'=4] {'fsdp'}, dimensions={0}, use_global_device_ids=true | all-gather | bytes 2304 | tf_op jit(solution)/shard_map/all_gather | solution.py:87
  47.1 11.1 %all-gather.15.cloned.1.call-done = bf16[1024,3072]{1,0:T(8,128)(2,1)} async-done(((bf16[128,3072]{1,0:T(8,128)(2,1)}), bf16[1024,3072]{1,0:T(8,128)(2,1)}) %all-gather.15.cloned.1.call-update) | async-done | bytes 6291472 | tf_op jit(solution)/shard_map/all_gather | solution.py:85
  77.1 75.7 %all-gather.4 = s32[4,1,384]{2,1,0:T(1,128)S(1)} all-gather(s32[1,1,384]{2,1,0:T(1,128)S(1)} %reshape.224), channel_id=1, replica_groups=mesh['fsdp'=8,'seq'=4] {'seq'}, dimensions={0}, use_global_device_ids=true | all-gather | bytes 7680 | tf_op jit(solution)/shard_map/all_gather | solution.py:91
  165.7 81.2 %while.26 = (s32[]{:T(128)}, bf16[2,768,4,64]{1,3,2,0:T(8,128)(2,1)}, f32[2,4,768]{2,1,0:T(4,128)S(1)}, s32[2]{0:T(128)S(1)}, bf16[2688,4,64]{0,2,1:T(8,128)(2,1...) while((s32[]{:T(128)}, ...), condition=%wide.region_5.6_spmd, body=%wide.region_2.5_spmd.sunk | while | flops 1582396416 | bytes 85851936 | solution.py:142
  170.6 12.1 %fusion.119 = (f32[4,768]{1,0:T(4,128)S(1)}, f32[4,768,1920]{2,1,0:T(8,128)}) fusion(pred[768,1920]{1,0:T(8,128)(4,1)S(1)} %broadcast_compare_fusion.4, bf16[2688,4,64]{0,2,1:T(8,128)(2,1)S(1)} %get-tuple-element.433, s32[]{:T(128)S(6)} %select_n.71, bf16[1536,4,64]{0,2,1:T(8,128)(2,1)} %get-tuple-element.432, s32[]{:T(128)S(6)} %select_n.72), kind=kOutput, calls=%fused_computation.3.clone.1 | convolution fusion | flops 772666368 | bytes 26456072 | tf_op jit(solution)/shard_map/while/body/eval_jaxpr/qhd,khd->hqk/dot_general | solution.py:120
  182.6 11.3 %fusion.120 = f32[4,768]{1,0:T(4,128)S(1)} fusion(f32[4,768,1920]{2,1,0:T(8,128)} %get-tuple-element.383, f32[4,768]{1,0:T(4,128)S(1)} %get-tuple-element.384, pred[768,1920]{1,0:T(8,128)(4,1)S(1)} %broadcast_compare_fusion.4), kind=kLoop, calls=%fused_computation.4.clone.1 | loop fusion | flops 23589888 | bytes 25092096 | tf_op jit(solution)/shard_map/while/body/eval_jaxpr/reduce_sum | solution.py:135
  193.9 11.6 %fusion.121 = bf16[2,768,4,64]{1,3,2,0:T(8,128)(2,1)S(1)} fusion(bf16[2,768,4,64]{1,3,2,0:T(8,128)(2,1)S(1)} %copy-done.17, s32[]{:T(128)S(6)} %copy.99, f32[4,768,1920]{2,1,0:T(8,128)} %get-tuple-element.383, f32[4,768]{1,0:T(4,128)S(1)} %fusion.120, f32[4,768]{1,0:T(4,128)S(1)} %get-tuple-element.384, ...), kind=kOutput, calls=%fused_computation.9.clone.1 | convolution fusion | flops 784662528 | bytes 26468360 | tf_op jit(solution)/shard_map/while/body/eval_jaxpr/hqk,khd->qhd/dot_general | solution.py:137
  211.3 11.9 %fusion.119 = (f32[4,768]{1,0:T(4,128)S(1)}, f32[4,768,1920]{2,1,0:T(8,128)}) fusion(pred[768,1920]{1,0:T(8,128)(4,1)S(1)} %broadcast_compare_fusion.4, bf16[2688,4,64]{0,2,1:T(8,128)(2,1)S(1)} %get-tuple-element.433, s32[]{:T(128)S(6)} %select_n.71, bf16[1536,4,64]{0,2,1:T(8,128)(2,1)} %get-tuple-element.432, s32[]{:T(128)S(6)} %select_n.72), kind=kOutput, calls=%fused_computation.3.clone.1 | convolution fusion | flops 772666368 | bytes 26456072 | tf_op jit(solution)/shard_map/while/body/eval_jaxpr/qhd,khd->hqk/dot_general | solution.py:120
  223.2 11.1 %fusion.120 = f32[4,768]{1,0:T(4,128)S(1)} fusion(f32[4,768,1920]{2,1,0:T(8,128)} %get-tuple-element.383, f32[4,768]{1,0:T(4,128)S(1)} %get-tuple-element.384, pred[768,1920]{1,0:T(8,128)(4,1)S(1)} %broadcast_compare_fusion.4), kind=kLoop, calls=%fused_computation.4.clone.1 | loop fusion | flops 23589888 | bytes 25092096 | tf_op jit(solution)/shard_map/while/body/eval_jaxpr/reduce_sum | solution.py:135
  234.3 11.7 %fusion.121 = bf16[2,768,4,64]{1,3,2,0:T(8,128)(2,1)S(1)} fusion(bf16[2,768,4,64]{1,3,2,0:T(8,128)(2,1)S(1)} %copy-done.17, s32[]{:T(128)S(6)} %copy.99, f32[4,768,1920]{2,1,0:T(8,128)} %get-tuple-element.383, f32[4,768]{1,0:T(4,128)S(1)} %fusion.120, f32[4,768]{1,0:T(4,128)S(1)} %get-tuple-element.384, ...), kind=kOutput, calls=%fused_computation.9.clone.1 | convolution fusion | flops 784662528 | bytes 26468360 | tf_op jit(solution)/shard_map/while/body/eval_jaxpr/hqk,khd->qhd/dot_general | solution.py:137
  298.2 20.9 %multiply_convert_fusion.1 = (bf16[384,4096]{1,0:T(8,128)(2,1)}, f32[384,4096]{1,0:T(8,128)}, f32[384,4096]{1,0:T(8,128)}) fusion(f32[4096]{0:T(1024)S(1)} %bitcast.133, bf16[1024,4096]{1,0:T(8,128)(2,1)} %all-gather.19.cloned.1.call-done, f32[384,1024]{1,0:T(8,128)} %copy-done.11, f32[1024]{0:T(1024)S(1)} %bitcast.142, f32[1024]{0:T(1024)S(1)} %bitcast.136, ...), kind=kOutput, calls=%fused_computation.56 | convolution fusion | flops 3327000576 | bytes 25717760 | tf_op jit(solution)/shard_map/dot_general | solution.py:160
  319.1 11.8 %fusion.81 = (bf16[4096]{0:T(1024)(128)(2,1)}, bf16[384,4096]{1,0:T(8,128)(2,1)S(1)}) fusion(f32[384,4096]{1,0:T(8,128)} %get-tuple-element.239, f32[384,4096]{1,0:T(8,128)} %get-tuple-element.250, bf16[4096,1024]{1,0:T(8,128)(2,1)} %all-gather.21.cloned.1.call-done, bf16[384,1024]{1,0:T(8,128)(2,1)} %param.35, f32[384]{0:T(512)S(1)} %compare_convert_fusion), kind=kOutput, calls=%fused_computation.137 | convolution fusion | flops 3245993984 | bytes 24913408 | tf_op jit(solution)/shard_map/dot_general | solution.py:27
  342.7 10.4 %convolution_convert_fusion.1 = bf16[1024,4096]{1,0:T(8,128)(2,1)} fusion(bf16[384,4096]{1,0:T(8,128)(2,1)} %copy-done.50, f32[384,1024]{1,0:T(8,128)} %copy-done.11, f32[1024]{0:T(1024)S(1)} %bitcast.143, f32[1024]{0:T(1024)S(1)} %bitcast.139, f32[384]{0:T(512)S(1)} %fusion.64, f32[384]{0:T(512)S(1)} %broadcast_multiply_fusion), kind=kOutput, calls=%fused_computation.53 | convolution fusion | flops 3227385856 | bytes 13118464 | tf_op jit(solution)/shard_map/dot_general | solution.py:21
  362.1 10.0 %convolution_convert_fusion = bf16[4096,1024]{1,0:T(8,128)(2,1)} fusion(bf16[384,4096]{1,0:T(8,128)(2,1)} %get-tuple-element.238, bf16[384,1024]{1,0:T(8,128)(2,1)} %param.35, f32[384]{0:T(512)S(1)} %compare_convert_fusion), kind=kOutput, calls=%fused_computation.52 | convolution fusion | flops 3226599424 | bytes 12322304 | tf_op jit(solution)/shard_map/dot_general | solution.py:21
  372.1 10.6 %all-to-all-done.2 = bf16[384,4,256]{2,0,1:T(8,128)(2,1)} async-done(((bf16[384,4,256]{2,0,1:T(8,128)(2,1)}), bf16[384,4,256]{2,0,1:T(8,128)(2,1)}, u32[]{:S(2)}, u32[]{:S(2)}) %all-to-all-start.2) | async-done | bytes 786464 | tf_op jit(solution)/shard_map/all_to_all | solution.py:188
  390.8 214.2 %while.27 = (s32[]{:T(128)}, f32[2688,4,64]{0,2,1:T(8,128)}, f32[2688,4,64]{0,2,1:T(8,128)}, bf16[2,768,4,64]{1,3,2,0:T(8,128)(2,1)}, s32[2]{0:T(128)S(1)}, /*in...) while((s32[]{:T(128)}, f32[2688,4,64]{0,2,1:T(8,128)}, ...), condition=%wide.region_12.13_spmd, body=%wide.region_10.12_spmd.sunk | while | flops 3866489856 | bytes 287363040 | solution.py:224
  394.9 13.9 %fusion.130 = f32[4,768,1920]{2,1,0:T(8,128)} fusion(bf16[2688,4,64]{0,2,1:T(8,128)(2,1)S(1)} %get-tuple-element.478, s32[]{:T(128)S(6)} %select_n.76, bf16[1536,4,64]{0,2,1:T(8,128)(2,1)} %get-tuple-element.475, s32[]{:T(128)S(6)} %select_n.77), kind=kOutput, calls=%fused_computation.37.clone.1 | convolution fusion | flops 754974720 | bytes 24969224 | tf_op jit(solution)/shard_map/while/body/eval_jaxpr/qhd,khd->hqk/dot_general | solution.py:120
  409.9 22.2 %multiply_reduce_fusion.5 = (f32[4,768]{1,0:T(4,128)S(1)}, f32[4,768,1920]{2,1,0:T(8,128)}) fusion(f32[4,768,1920]{2,1,0:T(8,128)} %fusion.130, f32[4,768]{1,0:T(4,128)S(1)} %dynamic-slice_bitcast_fusion.2, pred[768,1920]{1,0:T(8,128)(4,1)S(1)} %broadcast_compare_fusion.5, bf16[2688,4,64]{0,2,1:T(8,128)(2,1)S(1)} %get-tuple-element.481, ...), kind=kOutput, calls=%fused_computation.20.clone.1 | convolution fusion | flops 784462848 | bytes 50061320 | tf_op jit(solution)/shard_map/while/body/eval_jaxpr/qhd,khd->hqk/dot_general | solution.py:202
  432.1 17.7 %multiply_convert_fusion.4 = bf16[4,768,1920]{2,1,0:T(8,128)(2,1)S(1)} fusion(f32[4,768,1920]{2,1,0:T(8,128)} %get-tuple-element.397, f32[4,768,1920]{2,1,0:T(8,128)} %fusion.130, f32[4,768]{1,0:T(4,128)S(1)} %get-tuple-element.398, f32[4,768]{1,0:T(4,128)S(1)} %dynamic-slice_bitcast_fusion.2, pred[768,1920]{1,0:T(8,128)(4,1)S(1)} %broadcast_compare_fusion.5), kind=kLoop, calls=%fused_computation.19.clone.1 | loop fusion | flops 35389440 | bytes 60481536 | tf_op jit(solution)/shard_map/while/body/eval_jaxpr/convert_element_type | solution.py:206
  456.1 10.0 %dynamic_update_slice.29 = f32[2688,4,64]{0,2,1:T(8,128)} dynamic-update-slice(f32[2688,4,64]{0,2,1:T(8,128)} %get-tuple-element.455, f32[1920,4,64]{0,2,1:T(8,128)S(1)} %fusion.131, s32[]{:T(128)S(6)} %select_n.76, s32[]{:T(128)} %constant.72.clone.1..sunk.1, s32[]{:T(128)} %constant.72.clone.1..sunk.1) | dynamic-update-slice | bytes 3932164 | tf_op jit(solution)/shard_map/while/body/eval_jaxpr/dynamic_update_slice | solution.py:45
  466.1 16.1 %fusion.132 = f32[1920,4,64]{0,2,1:T(8,128)S(1)} fusion(f32[4,768,1920]{2,1,0:T(8,128)} %fusion.130, f32[4,768]{1,0:T(4,128)S(1)} %dynamic-slice_bitcast_fusion.2, pred[768,1920]{1,0:T(8,128)(4,1)S(1)} %broadcast_compare_fusion.5, f32[2688,4,64]{0,2,1:T(8,128)} %get-tuple-element.456, s32[]{:T(128)S(6)} %select_n.76, ...), kind=kOutput, calls=%fused_computation.30.clone.1 | convolution fusion | flops 779059200 | bytes 29405192 | tf_op jit(solution)/shard_map/while/body/eval_jaxpr/hqk,qhd->khd/dot_general | solution.py:199
  482.2 10.2 %dynamic_update_slice.30 = f32[2688,4,64]{0,2,1:T(8,128)} dynamic-update-slice(f32[2688,4,64]{0,2,1:T(8,128)} %get-tuple-element.456, f32[1920,4,64]{0,2,1:T(8,128)S(1)} %fusion.132, s32[]{:T(128)S(6)} %select_n.76, s32[]{:T(128)} %constant.72.clone.1..sunk.1, s32[]{:T(128)} %constant.72.clone.1..sunk.1) | dynamic-update-slice | bytes 3932164 | tf_op jit(solution)/shard_map/while/body/eval_jaxpr/dynamic_update_slice | solution.py:45
  505.5 12.3 %fusion.130 = f32[4,768,1920]{2,1,0:T(8,128)} fusion(bf16[2688,4,64]{0,2,1:T(8,128)(2,1)S(1)} %get-tuple-element.478, s32[]{:T(128)S(6)} %select_n.76, bf16[1536,4,64]{0,2,1:T(8,128)(2,1)} %get-tuple-element.475, s32[]{:T(128)S(6)} %select_n.77), kind=kOutput, calls=%fused_computation.37.clone.1 | convolution fusion | flops 754974720 | bytes 24969224 | tf_op jit(solution)/shard_map/while/body/eval_jaxpr/qhd,khd->hqk/dot_general | solution.py:120
  519.0 22.2 %multiply_reduce_fusion.5 = (f32[4,768]{1,0:T(4,128)S(1)}, f32[4,768,1920]{2,1,0:T(8,128)}) fusion(f32[4,768,1920]{2,1,0:T(8,128)} %fusion.130, f32[4,768]{1,0:T(4,128)S(1)} %dynamic-slice_bitcast_fusion.2, pred[768,1920]{1,0:T(8,128)(4,1)S(1)} %broadcast_compare_fusion.5, bf16[2688,4,64]{0,2,1:T(8,128)(2,1)S(1)} %get-tuple-element.481, ...), kind=kOutput, calls=%fused_computation.20.clone.1 | convolution fusion | flops 784462848 | bytes 50061320 | tf_op jit(solution)/shard_map/while/body/eval_jaxpr/qhd,khd->hqk/dot_general | solution.py:202
  541.2 17.0 %multiply_convert_fusion.4 = bf16[4,768,1920]{2,1,0:T(8,128)(2,1)S(1)} fusion(f32[4,768,1920]{2,1,0:T(8,128)} %get-tuple-element.397, f32[4,768,1920]{2,1,0:T(8,128)} %fusion.130, f32[4,768]{1,0:T(4,128)S(1)} %get-tuple-element.398, f32[4,768]{1,0:T(4,128)S(1)} %dynamic-slice_bitcast_fusion.2, pred[768,1920]{1,0:T(8,128)(4,1)S(1)} %broadcast_compare_fusion.5), kind=kLoop, calls=%fused_computation.19.clone.1 | loop fusion | flops 35389440 | bytes 60481536 | tf_op jit(solution)/shard_map/while/body/eval_jaxpr/convert_element_type | solution.py:206
  574.0 12.3 %fusion.132 = f32[1920,4,64]{0,2,1:T(8,128)S(1)} fusion(f32[4,768,1920]{2,1,0:T(8,128)} %fusion.130, f32[4,768]{1,0:T(4,128)S(1)} %dynamic-slice_bitcast_fusion.2, pred[768,1920]{1,0:T(8,128)(4,1)S(1)} %broadcast_compare_fusion.5, f32[2688,4,64]{0,2,1:T(8,128)} %get-tuple-element.456, s32[]{:T(128)S(6)} %select_n.76, ...), kind=kOutput, calls=%fused_computation.30.clone.1 | convolution fusion | flops 779059200 | bytes 29405192 | tf_op jit(solution)/shard_map/while/body/eval_jaxpr/hqk,qhd->khd/dot_general | solution.py:199
  586.4 9.5 %dynamic_update_slice.30 = f32[2688,4,64]{0,2,1:T(8,128)} dynamic-update-slice(f32[2688,4,64]{0,2,1:T(8,128)} %get-tuple-element.456, f32[1920,4,64]{0,2,1:T(8,128)S(1)} %fusion.132, s32[]{:T(128)S(6)} %select_n.76, s32[]{:T(128)} %constant.72.clone.1..sunk.1, s32[]{:T(128)} %constant.72.clone.1..sunk.1) | dynamic-update-slice | bytes 3932164 | tf_op jit(solution)/shard_map/while/body/eval_jaxpr/dynamic_update_slice | solution.py:45
  621.4 74.2 %all-to-all-done.3 = bf16[1536,3,256]{2,1,0:T(4,128)(2,1)S(1)} async-done(((bf16[1536,3,256]{2,1,0:T(4,128)(2,1)}), bf16[1536,3,256]{2,1,0:T(4,128)(2,1)S(1)}, u32[]{:S(2)}, u32[]{:S(2)}) %all-to-all-start.3) | async-done | bytes 2359328 | tf_op jit(solution)/shard_map/all_to_all | solution.py:237
  738.2 28.6 %reduce-scatter.9.cloned.1.call-done = bf16[128,3072]{1,0:T(8,128)(2,1)} async-done(((bf16[1024,3072]{1,0:T(8,128)(2,1)}), bf16[128,3072]{1,0:T(8,128)(2,1)}) %reduce-scatter.9.cloned.1.call-update) | async-done | bytes 786448 | tf_op jit(solution)/shard_map/reduce_scatter | solution.py:256
  770.7 23.8 %all-reduce.21 = (bf16[1024]{0:T(1024)(128)(2,1)S(1)}, bf16[1024]{0:T(1024)(128)(2,1)S(1)}, bf16[1024]{0:T(1024)(128)(2,1)S(1)}, bf16[1024]{0:T(1024)(128)(2,1)S...) all-reduce(bf16[1024]{0:T(1024)(128)(2,1)S(1)} %get-tuple-element.1, ...), channel_id=2, replica_groups=mesh['fsdp'=8,'seq'=4] {'fsdp'}, use_global_device_ids=true, to_apply=%region_16.17.clone | all-reduce | flops 12288 | bytes 49152
  795.2 12.5 %all-reduce.22 = (bf16[128]{0:T(256)(128)(2,1)S(1)}, bf16[128]{0:T(256)(128)(2,1)S(1)}, bf16[128]{0:T(256)(128)(2,1)S(1)}, bf16[128]{0:T(256)(128)(2,1)S(1)}, bf...) all-reduce(bf16[128]{0:T(256)(128)(2,1)S(1)} %dynamic-slice.1, ...), channel_id=3, replica_groups=mesh['fsdp'=8,'seq'=4] {'seq'}, use_global_device_ids=true, to_apply=%region_17.18.clone | all-reduce | flops 1536 | bytes 6144
  826.1 22.4 %reduce-scatter.11.cloned.1.call-done = bf16[128,768]{1,0:T(8,128)(2,1)} async-done(((bf16[128,3072]{1,0:T(8,128)(2,1)}), bf16[128,768]{1,0:T(8,128)(2,1)}) %reduce-scatter.11.cloned.1.call-update) | async-done | bytes 196624 | tf_op jit(solution)/shard_map/reduce_scatter | solution.py:297
  (283 shorter events, 270.5 us)
Async XLA Ops:
  7.2 39.0 %copy-start.7 = (bf16[384,1024]{1,0:T(8,128)(2,1)S(1)}, bf16[384,1024]{1,0:T(8,128)(2,1)}, u32[]{:S(2)}) copy-start(bf16[384,1024]{1,0:T(8,128)(2,1)} %param.20) | copy-start | bytes 2359300
  7.2 51.0 %all-gather.15.cloned.1.call-start = ((), (), s32[]{:S(2)}) async-start(), calls=%async_computation.12 | async-start | bytes 7077888 | tf_op jit(solution)/shard_map/all_gather | solution.py:85
  7.9 285.7 %all-gather.17.cloned.1.call-start = ((), (), s32[]{:S(2)}) async-start(), calls=%async_computation.13 | async-start | bytes 2359296 | tf_op jit(solution)/shard_map/all_gather | solution.py:88
  8.7 289.5 %all-gather.19.cloned.1.call-start = ((), (), s32[]{:S(2)}) async-start(), calls=%async_computation.14 | async-start | bytes 9437184 | tf_op jit(solution)/shard_map/all_gather | solution.py:152
  36.2 22.0 %copy-start.38 = (f32[8,1,128]{2,1,0:T(1,128)}, f32[8,1,128]{2,1,0:T(1,128)S(1)}, u32[]{:S(2)}) copy-start(f32[8,1,128]{2,1,0:T(1,128)S(1)} %convert_element_type.226) | copy-start | bytes 12292
  71.8 81.2 %all-to-all-start = ((bf16[384,3,1024]{0,1,2:T(4,128)(2,1)}), bf16[384,3,1024]{0,1,2:T(4,128)(2,1)S(1)}, u32[]{:S(2)}, u32[]{:S(2)}) async-start(bf16[384,3,1024]{0,1,2:T(4,128)(2,1)} %copy.74), calls=%async_computation | async-start | bytes 6291456 | tf_op jit(solution)/shard_map/all_to_all | solution.py:105
  76.5 242.6 %all-gather.21.cloned.1.call-start = ((), (), s32[]{:S(2)}) async-start(), calls=%async_computation.15 | async-start | bytes 9437184 | tf_op jit(solution)/shard_map/all_gather | solution.py:154
  246.9 30.2 %copy-start.44 = (bf16[128]{0:T(256)(128)(2,1)S(1)}, bf16[128]{0:T(256)(128)(2,1)}, u32[]{:S(2)}) copy-start(bf16[128]{0:T(256)(128)(2,1)} %param.30) | copy-start | bytes 772
  246.9 38.6 %copy-start.45 = (bf16[128]{0:T(256)(128)(2,1)S(1)}, bf16[128]{0:T(256)(128)(2,1)}, u32[]{:S(2)}) copy-start(bf16[128]{0:T(256)(128)(2,1)} %param.29) | copy-start | bytes 772
  246.9 46.7 %copy-start.37 = (s32[384]{0:T(512)S(1)}, s32[384]{0:T(512)}, u32[]{:S(2)}) copy-start(s32[384]{0:T(512)} %param.21) | copy-start | bytes 4612
  255.2 38.4 %all-to-all-start.1 = ((bf16[4,384,256]{1,2,0:T(8,128)(2,1)}), bf16[4,384,256]{1,2,0:T(8,128)(2,1)}, u32[]{:S(2)}, u32[]{:S(2)}) async-start(bf16[4,384,256]{1,2,0:T(8,128)(2,1)} %copy.81), calls=%async_computation.1 | async-start | bytes 1572864 | tf_op jit(solution)/shard_map/all_to_all | solution.py:144
  259.6 361.0 %reduce-scatter.13.cloned.1.call-start = ((), (), s32[]{:S(2)}) async-start(), calls=%async_computation.18 | async-start | bytes 2359296 | tf_op jit(solution)/shard_map/reduce_scatter | solution.py:265
  293.6 68.5 %copy-start.25 = (f32[384]{0:T(512)}, f32[384]{0:T(512)S(1)}, u32[]{:S(2)}) copy-start(f32[384]{0:T(512)S(1)} %compare_convert_fusion) | copy-start | bytes 4612
  342.6 364.0 %reduce-scatter.17.cloned.1.call-start = ((), (), s32[]{:S(2)}) async-start(), calls=%async_computation.20 | async-start | bytes 9437184 | tf_op jit(solution)/shard_map/reduce_scatter | solution.py:277
  357.1 25.7 %all-to-all-start.2 = ((bf16[384,4,256]{2,0,1:T(8,128)(2,1)}), bf16[384,4,256]{2,0,1:T(8,128)(2,1)}, u32[]{:S(2)}, u32[]{:S(2)}) async-start(bf16[384,4,256]{2,0,1:T(8,128)(2,1)} %bitcast.123), calls=%async_computation.2 | async-start | bytes 1572864 | tf_op jit(solution)/shard_map/all_to_all | solution.py:188
  362.0 345.1 %reduce-scatter.21.cloned.1.call-start = ((), (), s32[]{:S(2)}) async-start(), calls=%async_computation.22 | async-start | bytes 9437184 | tf_op jit(solution)/shard_map/reduce_scatter | solution.py:283
  432.1 22.0 %copy-start.3 = (f32[2688,4,64]{0,2,1:T(8,128)S(1)}, f32[2688,4,64]{0,2,1:T(8,128)}, u32[]{:S(2)}) copy-start(f32[2688,4,64]{0,2,1:T(8,128)} %get-tuple-element.455) | copy-start | bytes 8257540 | tf_op jit(solution)/shard_map/while
  432.1 22.0 %copy-start.6 = (bf16[1536,4,64]{0,2,1:T(8,128)(2,1)S(1)}, bf16[1536,4,64]{0,2,1:T(8,128)(2,1)}, u32[]{:S(2)}) copy-start(bf16[1536,4,64]{0,2,1:T(8,128)(2,1)} %get-tuple-element.475) | copy-start | bytes 2359300 | tf_op jit(solution)/shard_map/while
  616.9 78.7 %all-to-all-start.3 = ((bf16[1536,3,256]{2,1,0:T(4,128)(2,1)}), bf16[1536,3,256]{2,1,0:T(4,128)(2,1)S(1)}, u32[]{:S(2)}, u32[]{:S(2)}) async-start(bf16[1536,3,256]{2,1,0:T(4,128)(2,1)} %copy.85), calls=%async_computation.3 | async-start | bytes 6291456 | tf_op jit(solution)/shard_map/all_to_all | solution.py:237
  620.6 108.5 %reduce-scatter.15.cloned.1.call-start = ((), (), s32[]{:S(2)}) async-start(), calls=%async_computation.19 | async-start | bytes 327680 | tf_op jit(solution)/shard_map/reduce_scatter | solution.py:306
  621.3 145.4 %reduce-scatter.9.cloned.1.call-start = ((), (), s32[]{:S(2)}) async-start(), calls=%async_computation.16 | async-start | bytes 7077888 | tf_op jit(solution)/shard_map/reduce_scatter | solution.py:256
  706.5 107.4 %reduce-scatter.19.cloned.1.call-start = ((), (), s32[]{:S(2)}) async-start(), calls=%async_computation.21 | async-start | bytes 1310720 | tf_op jit(solution)/shard_map/reduce_scatter | solution.py:318
  707.1 117.3 %reduce-scatter.23.cloned.1.call-start = ((), (), s32[]{:S(2)}) async-start(), calls=%async_computation.23 | async-start | bytes 1310720 | tf_op jit(solution)/shard_map/reduce_scatter | solution.py:324
  707.8 140.7 %reduce-scatter.11.cloned.1.call-start = ((), (), s32[]{:S(2)}) async-start(), calls=%async_computation.17 | async-start | bytes 983040 | tf_op jit(solution)/shard_map/reduce_scatter | solution.py:297
  738.1 32.6 %copy-start.33 = (bf16[1024]{0:T(1024)(128)(2,1)S(1)}, bf16[1024]{0:T(1024)(128)(2,1)}, u32[]{:S(2)}) copy-start(bf16[1024]{0:T(1024)(128)(2,1)} %get-tuple-element.234) | copy-start | bytes 6148
  738.1 32.6 %copy-start.34 = (bf16[1024]{0:T(1024)(128)(2,1)S(1)}, bf16[1024]{0:T(1024)(128)(2,1)}, u32[]{:S(2)}) copy-start(bf16[1024]{0:T(1024)(128)(2,1)} %get-tuple-element.247) | copy-start | bytes 6148
  738.1 32.6 %copy-start.35 = (bf16[4096]{0:T(1024)(128)(2,1)S(1)}, bf16[4096]{0:T(1024)(128)(2,1)}, u32[]{:S(2)}) copy-start(bf16[4096]{0:T(1024)(128)(2,1)} %get-tuple-element.253) | copy-start | bytes 24580
  738.1 32.6 %copy-start.40 = (bf16[1024]{0:T(1024)(128)(2,1)S(1)}, bf16[1024]{0:T(1024)(128)(2,1)}, u32[]{:S(2)}) copy-start(bf16[1024]{0:T(1024)(128)(2,1)} %get-tuple-element.165) | copy-start | bytes 6148
  738.1 32.6 %copy-start.41 = (bf16[1024]{0:T(1024)(128)(2,1)S(1)}, bf16[1024]{0:T(1024)(128)(2,1)}, u32[]{:S(2)}) copy-start(bf16[1024]{0:T(1024)(128)(2,1)} %get-tuple-element.171) | copy-start | bytes 6148
  738.1 72.5 %copy-start.10 = (f32[384,1024]{1,0:T(8,128)S(1)}, f32[384,1024]{1,0:T(8,128)}, u32[]{:S(2)}) copy-start(f32[384,1024]{1,0:T(8,128)} %copy-done.9) | copy-start | bytes 4718596
  738.1 72.5 %copy-start.16 = (bf16[384,1024]{1,0:T(8,128)(2,1)S(1)}, bf16[384,1024]{1,0:T(8,128)(2,1)}, u32[]{:S(2)}) copy-start(bf16[384,1024]{1,0:T(8,128)(2,1)} %param.35) | copy-start | bytes 2359300
  738.1 72.5 %copy-start.28 = (f32[384]{0:T(512)S(1)}, f32[384]{0:T(512)}, u32[]{:S(2)}) copy-start(f32[384]{0:T(512)} %copy-done.27) | copy-start | bytes 4612
  (44 other events, 383.7 us)
Sparse Core Ops, SparseCore 0:
  9.9 48.2 all-gather.14
  60.1 27.8 all-gather.16
  89.9 54.3 all-gather.18
  146.1 54.3 all-gather.20
  342.7 41.5 reduce-scatter.12
  388.1 71.2 reduce-scatter.16
  462.8 71.2 reduce-scatter.20
  623.8 27.1 reduce-scatter.14
  706.6 60.0 reduce-scatter.8
  769.0 27.1 reduce-scatter.18
  798.5 25.8 reduce-scatter.22
  826.6 21.8 reduce-scatter.10
where the time goes:
time: 865 us; the launch traced here: 857 us
  matrix products  265 us (31%)
  blocking collectives  190 us (22%)
  waiting for transfers between devices  160 us (18%)
  local copies, waits for them, and re-layouts  110 us (13%)
  other arithmetic  83 us (10%)
  starting transfers between devices  18.2 us (2%)
  between operations  17.8 us (2%)
  loops' own time  13.6 us (2%)
    all_gather x1, blocking collectives, shards(): span_labels = lax.all_gather(segment_ids, 'seq', axis=0, tiled=True)  75.7 us
    all_to_all x1, waiting for transfers between devices, shards(): lax.all_to_all(head_grads, 'seq', split_axis=0, concat_axis=2, tiled=True)  74.2 us
    dot_general x4, matrix products, block_scores(): jnp.einsum('qhd,khd->hqk', query_block, key_window, preferred_element_typ...  50.2 us
    dot_general x2, matrix products, block_backward(): jnp.einsum('qhd,khd->hqk', grad_block, value_window, preferred_element_ty...  44.4 us
    dynamic_update_slice x4, local copies, waits for them, and re-layouts, add_window(): return lax.dynamic_update_slice_in_dim(total, current + delta, start, 0)  39.2 us
    unnamed x2, blocking collectives  36.3 us
    convert_element_type x2, other arithmetic, block_backward(): grad_scores = (probs_full * (grad_probs - row_inner)).astype(jnp.bfloat16)  34.8 us
    dot_general x4, matrix products, contract_rows(): lax.dot_general(left, right, (((0,), (0,)), ((), ())), preferred_element_...  30.1 us
  transfers between devices with their start and end apart: 16, of which 6 were waited for; matrix products, arithmetic and copies ran while one was open for 49% of the time, Pallas kernels for 0%

commit v1 on v0

--- a/solution.py
+++ b/solution.py
@@ -1,3 +1,4 @@
+import functools
 from functools import partial
 import jax
 import jax.numpy as jnp
@@ -8,6 +9,34 @@
 LEN = 577
 norm_eps = 1e-06
 masked_score = -1000000000.0
+
+
+def feed_strips_all_in(frame, row_axis):
+    wide_out = jax.lax.axis_size(row_axis)
+    x_now = jax.lax.axis_index(row_axis)
+    upper, tmp = (wide_out, x_now)
+    current_block = frame.shape[1] // upper
+    p_next = list(frame.shape)
+    p_next[1] = current_block
+    all_rows = p_next[0]
+    p_next[0] = all_rows * upper
+    ready = jnp.zeros(p_next, frame.dtype)
+    tick = 0
+    while tick < upper:
+        f_now = lax.dynamic_slice_in_dim(frame, (tmp ^ tick) * current_block, current_block, axis=1)
+        if tick:
+            trail = []
+            at = 0
+            while at < upper:
+                trail.append((at, at ^ tick))
+                at += 1
+            f_now = jax.lax.ppermute(f_now, row_axis, trail)
+        ready = lax.dynamic_update_slice_in_dim(ready, f_now, (tmp ^ tick) * all_rows, axis=0)
+        tick += 1
+    return ready
+
+
+_post_meshes = functools.partial(feed_strips_all_in, row_axis="seq")
 
 
 def normalize(values, gain, shift):
@@ -185,9 +214,7 @@
     out_bias_part = column_sum(grad_mixed)
     w_out_part = weight_grad(attended, grad_mixed)
     grad_attended = times_transposed(grad_mixed, attn_set[5]).astype(jnp.bfloat16)
-    grad_heads = lax.all_to_all(
-        grad_attended, "seq", split_axis=1, concat_axis=0, tiled=True
-    ).reshape(span_rows, local_heads, HD)
+    grad_heads = _post_meshes(grad_attended).reshape(span_rows, local_heads, HD)
 
     def block_backward(running, inputs_block):
         key_total, value_total = running

time: 865 us -> 856 us (0.990)
    all_to_all x1 -> x0, waiting for transfers between devices: 10.6 us -> none  [shards(): lax.all_to_all(grad_attended, 'seq', split_axis=1, concat_axis=0, tiled=T...]
  transfers between devices with their start and end apart: 16 -> 18, of which waited for: 6 -> 6; matrix products, arithmetic and copies ran while one was open for 49% -> 49% of each run, Pallas kernels for 0% -> 0%
where the time goes in v1:
time: 856 us; the launch traced here: 849 us
  matrix products  261 us (30%)
  blocking collectives  189 us (22%)
  waiting for transfers between devices  155 us (18%)
  local copies, waits for them, and re-layouts  111 us (13%)
  other arithmetic  82.6 us (10%)
  starting transfers between devices  18.1 us (2%)
  between operations  17.8 us (2%)
  loops' own time  13.6 us (2%)
    all_gather x1, blocking collectives, shards(): span_labels = lax.all_gather(segment_ids, 'seq', axis=0, tiled=True)  75.7 us
    all_to_all x1, waiting for transfers between devices, shards(): lax.all_to_all(head_grads, 'seq', split_axis=0, concat_axis=2, tiled=True)  72.7 us
    dot_general x4, matrix products, block_scores(): jnp.einsum('qhd,khd->hqk', query_block, key_window, preferred_element_typ...  51.7 us
    dot_general x2, matrix products, block_backward(): jnp.einsum('qhd,khd->hqk', grad_block, value_window, preferred_element_ty...  44.3 us
    dynamic_update_slice x4, local copies, waits for them, and re-layouts, add_window(): return lax.dynamic_update_slice_in_dim(total, current + delta, start, 0)  39.3 us
    unnamed x2, blocking collectives  36.3 us
    convert_element_type x2, other arithmetic, block_backward(): grad_scores = (probs_full * (grad_probs - row_inner)).astype(jnp.bfloat16)  34.4 us
    reduce_scatter x1, waiting for transfers between devices, shards(): lax.psum_scatter(w_qkv_part.astype(jnp.bfloat16), 'fsdp', scatter_dimensi...  28.3 us
  transfers between devices with their start and end apart: 18, of which 6 were waited for; matrix products, arithmetic and copies ran while one was open for 49% of the time, Pallas kernels for 0%

profile of v1, /device:TPU:0, one launch (start us, length us, event | category | flops | bytes accessed | tf_op | source)
XLA Modules:
  0.0 848.6 jit_solution(2262013457316206588)
XLA Ops:
  9.4 10.3 %all-gather.3 = bf16[8,1,128]{2,1,0:T(2,128)(2,1)S(1)} all-gather(bf16[1,1,128]{2,1,0:T(2,128)(2,1)} %bitcast.138), channel_id=1, replica_groups=mesh['fsdp'=8,'seq'=4] {'fsdp'}, dimensions={0}, use_global_device_ids=true | all-gather | bytes 2304 | tf_op jit(solution)/shard_map/all_gather | solution.py:116
  47.1 11.1 %all-gather.15.cloned.1.call-done = bf16[1024,3072]{1,0:T(8,128)(2,1)} async-done(((bf16[128,3072]{1,0:T(8,128)(2,1)}), bf16[1024,3072]{1,0:T(8,128)(2,1)}) %all-gather.15.cloned.1.call-update) | async-done | bytes 6291472 | tf_op jit(solution)/shard_map/all_gather | solution.py:114
  77.1 75.7 %all-gather.4 = s32[4,1,384]{2,1,0:T(1,128)S(1)} all-gather(s32[1,1,384]{2,1,0:T(1,128)S(1)} %reshape.220), channel_id=1, replica_groups=mesh['fsdp'=8,'seq'=4] {'seq'}, dimensions={0}, use_global_device_ids=true | all-gather | bytes 7680 | tf_op jit(solution)/shard_map/all_gather | solution.py:120
  165.7 80.9 %while.26 = (s32[]{:T(128)}, bf16[2,768,4,64]{1,3,2,0:T(8,128)(2,1)}, f32[2,4,768]{2,1,0:T(4,128)S(1)}, s32[2]{0:T(128)S(1)}, bf16[2688,4,64]{0,2,1:T(8,128)(2,1...) while((s32[]{:T(128)}, ...), condition=%wide.region_5.6_spmd, body=%wide.region_2.5_spmd.sunk | while | flops 1582396416 | bytes 85851936 | solution.py:171
  170.6 11.8 %fusion.119 = (f32[4,768]{1,0:T(4,128)S(1)}, f32[4,768,1920]{2,1,0:T(8,128)}) fusion(pred[768,1920]{1,0:T(8,128)(4,1)S(1)} %broadcast_compare_fusion.4, bf16[2688,4,64]{0,2,1:T(8,128)(2,1)S(1)} %get-tuple-element.425, s32[]{:T(128)S(6)} %select_n.103, bf16[1536,4,64]{0,2,1:T(8,128)(2,1)} %get-tuple-element.424, s32[]{:T(128)S(6)} %select_n.104), kind=kOutput, calls=%fused_computation.3.clone.1 | convolution fusion | flops 772666368 | bytes 26456072 | tf_op jit(solution)/shard_map/while/body/eval_jaxpr/qhd,khd->hqk/dot_general | solution.py:149
  182.5 11.2 %fusion.120 = f32[4,768]{1,0:T(4,128)S(1)} fusion(f32[4,768,1920]{2,1,0:T(8,128)} %get-tuple-element.375, f32[4,768]{1,0:T(4,128)S(1)} %get-tuple-element.376, pred[768,1920]{1,0:T(8,128)(4,1)S(1)} %broadcast_compare_fusion.4), kind=kLoop, calls=%fused_computation.4.clone.1 | loop fusion | flops 23589888 | bytes 25092096 | tf_op jit(solution)/shard_map/while/body/eval_jaxpr/reduce_sum | solution.py:164
  193.7 11.7 %fusion.121 = bf16[2,768,4,64]{1,3,2,0:T(8,128)(2,1)S(1)} fusion(bf16[2,768,4,64]{1,3,2,0:T(8,128)(2,1)S(1)} %copy-done.19, s32[]{:T(128)S(6)} %copy.100, f32[4,768,1920]{2,1,0:T(8,128)} %get-tuple-element.375, f32[4,768]{1,0:T(4,128)S(1)} %fusion.120, f32[4,768]{1,0:T(4,128)S(1)} %get-tuple-element.376, ...), kind=kOutput, calls=%fused_computation.9.clone.1 | convolution fusion | flops 784662528 | bytes 26468360 | tf_op jit(solution)/shard_map/while/body/eval_jaxpr/hqk,khd->qhd/dot_general | solution.py:166
  211.1 11.8 %fusion.119 = (f32[4,768]{1,0:T(4,128)S(1)}, f32[4,768,1920]{2,1,0:T(8,128)}) fusion(pred[768,1920]{1,0:T(8,128)(4,1)S(1)} %broadcast_compare_fusion.4, bf16[2688,4,64]{0,2,1:T(8,128)(2,1)S(1)} %get-tuple-element.425, s32[]{:T(128)S(6)} %select_n.103, bf16[1536,4,64]{0,2,1:T(8,128)(2,1)} %get-tuple-element.424, s32[]{:T(128)S(6)} %select_n.104), kind=kOutput, calls=%fused_computation.3.clone.1 | convolution fusion | flops 772666368 | bytes 26456072 | tf_op jit(solution)/shard_map/while/body/eval_jaxpr/qhd,khd->hqk/dot_general | solution.py:149
  222.9 11.1 %fusion.120 = f32[4,768]{1,0:T(4,128)S(1)} fusion(f32[4,768,1920]{2,1,0:T(8,128)} %get-tuple-element.375, f32[4,768]{1,0:T(4,128)S(1)} %get-tuple-element.376, pred[768,1920]{1,0:T(8,128)(4,1)S(1)} %broadcast_compare_fusion.4), kind=kLoop, calls=%fused_computation.4.clone.1 | loop fusion | flops 23589888 | bytes 25092096 | tf_op jit(solution)/shard_map/while/body/eval_jaxpr/reduce_sum | solution.py:164
  234.0 11.7 %fusion.121 = bf16[2,768,4,64]{1,3,2,0:T(8,128)(2,1)S(1)} fusion(bf16[2,768,4,64]{1,3,2,0:T(8,128)(2,1)S(1)} %copy-done.19, s32[]{:T(128)S(6)} %copy.100, f32[4,768,1920]{2,1,0:T(8,128)} %get-tuple-element.375, f32[4,768]{1,0:T(4,128)S(1)} %fusion.120, f32[4,768]{1,0:T(4,128)S(1)} %get-tuple-element.376, ...), kind=kOutput, calls=%fused_computation.9.clone.1 | convolution fusion | flops 784662528 | bytes 26468360 | tf_op jit(solution)/shard_map/while/body/eval_jaxpr/hqk,khd->qhd/dot_general | solution.py:166
  298.0 21.1 %multiply_convert_fusion.1 = (bf16[384,4096]{1,0:T(8,128)(2,1)}, f32[384,4096]{1,0:T(8,128)}, f32[384,4096]{1,0:T(8,128)}) fusion(f32[4096]{0:T(1024)S(1)} %bitcast.126, bf16[1024,4096]{1,0:T(8,128)(2,1)} %all-gather.19.cloned.1.call-done, f32[384,1024]{1,0:T(8,128)} %copy-done.11, f32[1024]{0:T(1024)S(1)} %bitcast.135, f32[1024]{0:T(1024)S(1)} %bitcast.129, ...), kind=kOutput, calls=%fused_computation.56 | convolution fusion | flops 3327000576 | bytes 25717760 | tf_op jit(solution)/shard_map/dot_general | solution.py:189
  319.1 11.7 %fusion.81 = (bf16[4096]{0:T(1024)(128)(2,1)}, bf16[384,4096]{1,0:T(8,128)(2,1)S(1)}) fusion(f32[384,4096]{1,0:T(8,128)} %get-tuple-element.227, f32[384,4096]{1,0:T(8,128)} %get-tuple-element.242, bf16[4096,1024]{1,0:T(8,128)(2,1)} %all-gather.21.cloned.1.call-done, bf16[384,1024]{1,0:T(8,128)(2,1)} %param.35, f32[384]{0:T(512)S(1)} %compare_convert_fusion), kind=kOutput, calls=%fused_computation.143 | convolution fusion | flops 3245993984 | bytes 24913408 | tf_op jit(solution)/shard_map/dot_general | solution.py:56
  342.6 10.4 %convolution_convert_fusion.1 = bf16[1024,4096]{1,0:T(8,128)(2,1)} fusion(bf16[384,4096]{1,0:T(8,128)(2,1)} %copy-done.51, f32[384,1024]{1,0:T(8,128)} %copy-done.11, f32[1024]{0:T(1024)S(1)} %bitcast.136, f32[1024]{0:T(1024)S(1)} %bitcast.132, f32[384]{0:T(512)S(1)} %fusion.64, f32[384]{0:T(512)S(1)} %broadcast_multiply_fusion), kind=kOutput, calls=%fused_computation.53 | convolution fusion | flops 3227385856 | bytes 13118464 | tf_op jit(solution)/shard_map/dot_general | solution.py:50
  384.8 213.3 %while.27 = (s32[]{:T(128)}, f32[2688,4,64]{0,2,1:T(8,128)}, f32[2688,4,64]{0,2,1:T(8,128)}, bf16[2,768,4,64]{1,3,2,0:T(8,128)(2,1)}, s32[2]{0:T(128)S(1)}, /*in...) while((s32[]{:T(128)}, f32[2688,4,64]{0,2,1:T(8,128)}, ...), condition=%wide.region_12.13_spmd, body=%wide.region_10.12_spmd.sunk | while | flops 3866489856 | bytes 287363040 | solution.py:251
  388.9 15.7 %fusion.130 = f32[4,768,1920]{2,1,0:T(8,128)} fusion(bf16[2688,4,64]{0,2,1:T(8,128)(2,1)S(1)} %get-tuple-element.470, s32[]{:T(128)S(6)} %select_n.108, bf16[1536,4,64]{0,2,1:T(8,128)(2,1)} %get-tuple-element.467, s32[]{:T(128)S(6)} %select_n.109), kind=kOutput, calls=%fused_computation.37.clone.1 | convolution fusion | flops 754974720 | bytes 24969224 | tf_op jit(solution)/shard_map/while/body/eval_jaxpr/qhd,khd->hqk/dot_general | solution.py:149
  405.7 22.2 %multiply_reduce_fusion.5 = (f32[4,768]{1,0:T(4,128)S(1)}, f32[4,768,1920]{2,1,0:T(8,128)}) fusion(f32[4,768,1920]{2,1,0:T(8,128)} %fusion.130, f32[4,768]{1,0:T(4,128)S(1)} %dynamic-slice_bitcast_fusion.2, pred[768,1920]{1,0:T(8,128)(4,1)S(1)} %broadcast_compare_fusion.5, bf16[2688,4,64]{0,2,1:T(8,128)(2,1)S(1)} %get-tuple-element.473, ...), kind=kOutput, calls=%fused_computation.20.clone.1 | convolution fusion | flops 784462848 | bytes 50061320 | tf_op jit(solution)/shard_map/while/body/eval_jaxpr/qhd,khd->hqk/dot_general | solution.py:229
  427.9 17.4 %multiply_convert_fusion.4 = bf16[4,768,1920]{2,1,0:T(8,128)(2,1)S(1)} fusion(f32[4,768,1920]{2,1,0:T(8,128)} %get-tuple-element.389, f32[4,768,1920]{2,1,0:T(8,128)} %fusion.130, f32[4,768]{1,0:T(4,128)S(1)} %get-tuple-element.390, f32[4,768]{1,0:T(4,128)S(1)} %dynamic-slice_bitcast_fusion.2, pred[768,1920]{1,0:T(8,128)(4,1)S(1)} %broadcast_compare_fusion.5), kind=kLoop, calls=%fused_computation.19.clone.1 | loop fusion | flops 35389440 | bytes 60481536 | tf_op jit(solution)/shard_map/while/body/eval_jaxpr/convert_element_type | solution.py:233
  451.5 10.0 %dynamic_update_slice.49 = f32[2688,4,64]{0,2,1:T(8,128)} dynamic-update-slice(f32[2688,4,64]{0,2,1:T(8,128)} %get-tuple-element.447, f32[1920,4,64]{0,2,1:T(8,128)S(1)} %fusion.131, s32[]{:T(128)S(6)} %select_n.108, s32[]{:T(128)} %constant.80.clone.1..sunk.1, s32[]{:T(128)} %constant.80.clone.1..sunk.1) | dynamic-update-slice | bytes 3932164 | tf_op jit(solution)/shard_map/while/body/eval_jaxpr/dynamic_update_slice | solution.py:74
  461.6 13.2 %fusion.132 = f32[1920,4,64]{0,2,1:T(8,128)S(1)} fusion(f32[4,768,1920]{2,1,0:T(8,128)} %fusion.130, f32[4,768]{1,0:T(4,128)S(1)} %dynamic-slice_bitcast_fusion.2, pred[768,1920]{1,0:T(8,128)(4,1)S(1)} %broadcast_compare_fusion.5, f32[2688,4,64]{0,2,1:T(8,128)} %get-tuple-element.448, s32[]{:T(128)S(6)} %select_n.108, ...), kind=kOutput, calls=%fused_computation.30.clone.1 | convolution fusion | flops 779059200 | bytes 29405192 | tf_op jit(solution)/shard_map/while/body/eval_jaxpr/hqk,qhd->khd/dot_general | solution.py:226
  474.7 10.3 %dynamic_update_slice.50 = f32[2688,4,64]{0,2,1:T(8,128)} dynamic-update-slice(f32[2688,4,64]{0,2,1:T(8,128)} %get-tuple-element.448, f32[1920,4,64]{0,2,1:T(8,128)S(1)} %fusion.132, s32[]{:T(128)S(6)} %select_n.108, s32[]{:T(128)} %constant.80.clone.1..sunk.1, s32[]{:T(128)} %constant.80.clone.1..sunk.1) | dynamic-update-slice | bytes 3932164 | tf_op jit(solution)/shard_map/while/body/eval_jaxpr/dynamic_update_slice | solution.py:74
  485.1 9.6 %fusion.133 = bf16[2,768,4,64]{1,3,2,0:T(8,128)(2,1)} fusion(bf16[2,768,4,64]{1,3,2,0:T(8,128)(2,1)} %get-tuple-element.449, s32[]{:T(128)S(6)} %copy.114, bf16[4,768,1920]{2,1,0:T(8,128)(2,1)} %copy-done, bf16[2688,4,64]{0,2,1:T(8,128)(2,1)S(1)} %copy-done.2, s32[]{:T(128)S(6)} %select_n.108), kind=kOutput, calls=%fused_computation.33.clone.1 | convolution fusion | flops 755171328 | bytes 13565960 | tf_op jit(solution)/shard_map/while/body/eval_jaxpr/hqk,khd->qhd/dot_general | solution.py:235
  498.6 12.4 %fusion.130 = f32[4,768,1920]{2,1,0:T(8,128)} fusion(bf16[2688,4,64]{0,2,1:T(8,128)(2,1)S(1)} %get-tuple-element.470, s32[]{:T(128)S(6)} %select_n.108, bf16[1536,4,64]{0,2,1:T(8,128)(2,1)} %get-tuple-element.467, s32[]{:T(128)S(6)} %select_n.109), kind=kOutput, calls=%fused_computation.37.clone.1 | convolution fusion | flops 754974720 | bytes 24969224 | tf_op jit(solution)/shard_map/while/body/eval_jaxpr/qhd,khd->hqk/dot_general | solution.py:149
  512.1 22.1 %multiply_reduce_fusion.5 = (f32[4,768]{1,0:T(4,128)S(1)}, f32[4,768,1920]{2,1,0:T(8,128)}) fusion(f32[4,768,1920]{2,1,0:T(8,128)} %fusion.130, f32[4,768]{1,0:T(4,128)S(1)} %dynamic-slice_bitcast_fusion.2, pred[768,1920]{1,0:T(8,128)(4,1)S(1)} %broadcast_compare_fusion.5, bf16[2688,4,64]{0,2,1:T(8,128)(2,1)S(1)} %get-tuple-element.473, ...), kind=kOutput, calls=%fused_computation.20.clone.1 | convolution fusion | flops 784462848 | bytes 50061320 | tf_op jit(solution)/shard_map/while/body/eval_jaxpr/qhd,khd->hqk/dot_general | solution.py:229
  534.3 17.0 %multiply_convert_fusion.4 = bf16[4,768,1920]{2,1,0:T(8,128)(2,1)S(1)} fusion(f32[4,768,1920]{2,1,0:T(8,128)} %get-tuple-element.389, f32[4,768,1920]{2,1,0:T(8,128)} %fusion.130, f32[4,768]{1,0:T(4,128)S(1)} %get-tuple-element.390, f32[4,768]{1,0:T(4,128)S(1)} %dynamic-slice_bitcast_fusion.2, pred[768,1920]{1,0:T(8,128)(4,1)S(1)} %broadcast_compare_fusion.5), kind=kLoop, calls=%fused_computation.19.clone.1 | loop fusion | flops 35389440 | bytes 60481536 | tf_op jit(solution)/shard_map/while/body/eval_jaxpr/convert_element_type | solution.py:233
  557.7 9.4 %dynamic_update_slice.49 = f32[2688,4,64]{0,2,1:T(8,128)} dynamic-update-slice(f32[2688,4,64]{0,2,1:T(8,128)} %get-tuple-element.447, f32[1920,4,64]{0,2,1:T(8,128)S(1)} %fusion.131, s32[]{:T(128)S(6)} %select_n.108, s32[]{:T(128)} %constant.80.clone.1..sunk.1, s32[]{:T(128)} %constant.80.clone.1..sunk.1) | dynamic-update-slice | bytes 3932164 | tf_op jit(solution)/shard_map/while/body/eval_jaxpr/dynamic_update_slice | solution.py:74
  567.1 12.4 %fusion.132 = f32[1920,4,64]{0,2,1:T(8,128)S(1)} fusion(f32[4,768,1920]{2,1,0:T(8,128)} %fusion.130, f32[4,768]{1,0:T(4,128)S(1)} %dynamic-slice_bitcast_fusion.2, pred[768,1920]{1,0:T(8,128)(4,1)S(1)} %broadcast_compare_fusion.5, f32[2688,4,64]{0,2,1:T(8,128)} %get-tuple-element.448, s32[]{:T(128)S(6)} %select_n.108, ...), kind=kOutput, calls=%fused_computation.30.clone.1 | convolution fusion | flops 779059200 | bytes 29405192 | tf_op jit(solution)/shard_map/while/body/eval_jaxpr/hqk,qhd->khd/dot_general | solution.py:226
  579.5 9.5 %dynamic_update_slice.50 = f32[2688,4,64]{0,2,1:T(8,128)} dynamic-update-slice(f32[2688,4,64]{0,2,1:T(8,128)} %get-tuple-element.448, f32[1920,4,64]{0,2,1:T(8,128)S(1)} %fusion.132, s32[]{:T(128)S(6)} %select_n.108, s32[]{:T(128)} %constant.80.clone.1..sunk.1, s32[]{:T(128)} %constant.80.clone.1..sunk.1) | dynamic-update-slice | bytes 3932164 | tf_op jit(solution)/shard_map/while/body/eval_jaxpr/dynamic_update_slice | solution.py:74
  615.0 72.7 %all-to-all-done.2 = bf16[1536,3,256]{2,1,0:T(4,128)(2,1)S(1)} async-done(((bf16[1536,3,256]{2,1,0:T(4,128)(2,1)}), bf16[1536,3,256]{2,1,0:T(4,128)(2,1)S(1)}, u32[]{:S(2)}, u32[]{:S(2)}) %all-to-all-start.2) | async-done | bytes 2359328 | tf_op jit(solution)/shard_map/all_to_all | solution.py:264
  729.6 28.3 %reduce-scatter.9.cloned.1.call-done = bf16[128,3072]{1,0:T(8,128)(2,1)} async-done(((bf16[1024,3072]{1,0:T(8,128)(2,1)}), bf16[128,3072]{1,0:T(8,128)(2,1)}) %reduce-scatter.9.cloned.1.call-update) | async-done | bytes 786448 | tf_op jit(solution)/shard_map/reduce_scatter | solution.py:283
  761.8 23.8 %all-reduce.21 = (bf16[1024]{0:T(1024)(128)(2,1)S(1)}, bf16[1024]{0:T(1024)(128)(2,1)S(1)}, bf16[1024]{0:T(1024)(128)(2,1)S(1)}, bf16[1024]{0:T(1024)(128)(2,1)S...) all-reduce(bf16[1024]{0:T(1024)(128)(2,1)S(1)} %get-tuple-element.1, ...), channel_id=2, replica_groups=mesh['fsdp'=8,'seq'=4] {'fsdp'}, use_global_device_ids=true, to_apply=%region_16.17.clone | all-reduce | flops 12288 | bytes 49152
  786.3 12.5 %all-reduce.22 = (bf16[128]{0:T(256)(128)(2,1)S(1)}, bf16[128]{0:T(256)(128)(2,1)S(1)}, bf16[128]{0:T(256)(128)(2,1)S(1)}, bf16[128]{0:T(256)(128)(2,1)S(1)}, bf...) all-reduce(bf16[128]{0:T(256)(128)(2,1)S(1)} %dynamic-slice.1, ...), channel_id=3, replica_groups=mesh['fsdp'=8,'seq'=4] {'seq'}, use_global_device_ids=true, to_apply=%region_17.18.clone | all-reduce | flops 1536 | bytes 6144
  817.3 22.4 %reduce-scatter.11.cloned.1.call-done = bf16[128,768]{1,0:T(8,128)(2,1)} async-done(((bf16[128,3072]{1,0:T(8,128)(2,1)}), bf16[128,768]{1,0:T(8,128)(2,1)}) %reduce-scatter.11.cloned.1.call-update) | async-done | bytes 196624 | tf_op jit(solution)/shard_map/reduce_scatter | solution.py:324
  (295 shorter events, 266.5 us)
Async XLA Ops:
  7.2 39.0 %copy-start.7 = (bf16[384,1024]{1,0:T(8,128)(2,1)S(1)}, bf16[384,1024]{1,0:T(8,128)(2,1)}, u32[]{:S(2)}) copy-start(bf16[384,1024]{1,0:T(8,128)(2,1)} %param.20) | copy-start | bytes 2359300
  7.2 51.0 %all-gather.15.cloned.1.call-start = ((), (), s32[]{:S(2)}) async-start(), calls=%async_computation.11 | async-start | bytes 7077888 | tf_op jit(solution)/shard_map/all_gather | solution.py:114
  7.9 285.5 %all-gather.17.cloned.1.call-start = ((), (), s32[]{:S(2)}) async-start(), calls=%async_computation.12 | async-start | bytes 2359296 | tf_op jit(solution)/shard_map/all_gather | solution.py:117
  8.7 289.3 %all-gather.19.cloned.1.call-start = ((), (), s32[]{:S(2)}) async-start(), calls=%async_computation.13 | async-start | bytes 9437184 | tf_op jit(solution)/shard_map/all_gather | solution.py:181
  36.2 22.0 %copy-start.39 = (f32[8,1,128]{2,1,0:T(1,128)}, f32[8,1,128]{2,1,0:T(1,128)S(1)}, u32[]{:S(2)}) copy-start(f32[8,1,128]{2,1,0:T(1,128)S(1)} %convert_element_type.226) | copy-start | bytes 12292
  71.8 81.2 %all-to-all-start = ((bf16[384,3,1024]{0,1,2:T(4,128)(2,1)}), bf16[384,3,1024]{0,1,2:T(4,128)(2,1)S(1)}, u32[]{:S(2)}, u32[]{:S(2)}) async-start(bf16[384,3,1024]{0,1,2:T(4,128)(2,1)} %copy.78), calls=%async_computation | async-start | bytes 6291456 | tf_op jit(solution)/shard_map/all_to_all | solution.py:134
  76.5 242.6 %all-gather.21.cloned.1.call-start = ((), (), s32[]{:S(2)}) async-start(), calls=%async_computation.14 | async-start | bytes 9437184 | tf_op jit(solution)/shard_map/all_gather | solution.py:183
  246.6 30.2 %copy-start.45 = (bf16[128]{0:T(256)(128)(2,1)S(1)}, bf16[128]{0:T(256)(128)(2,1)}, u32[]{:S(2)}) copy-start(bf16[128]{0:T(256)(128)(2,1)} %param.30) | copy-start | bytes 772
  246.6 38.6 %copy-start.46 = (bf16[128]{0:T(256)(128)(2,1)S(1)}, bf16[128]{0:T(256)(128)(2,1)}, u32[]{:S(2)}) copy-start(bf16[128]{0:T(256)(128)(2,1)} %param.29) | copy-start | bytes 772
  246.6 46.7 %copy-start.38 = (s32[384]{0:T(512)S(1)}, s32[384]{0:T(512)}, u32[]{:S(2)}) copy-start(s32[384]{0:T(512)} %param.21) | copy-start | bytes 4612
  254.9 38.5 %all-to-all-start.1 = ((bf16[4,384,256]{1,2,0:T(8,128)(2,1)}), bf16[4,384,256]{1,2,0:T(8,128)(2,1)}, u32[]{:S(2)}, u32[]{:S(2)}) async-start(bf16[4,384,256]{1,2,0:T(8,128)(2,1)} %copy.85), calls=%async_computation.1 | async-start | bytes 1572864 | tf_op jit(solution)/shard_map/all_to_all | solution.py:173
  259.3 354.8 %reduce-scatter.13.cloned.1.call-start = ((), (), s32[]{:S(2)}) async-start(), calls=%async_computation.17 | async-start | bytes 2359296 | tf_op jit(solution)/shard_map/reduce_scatter | solution.py:292
  293.4 69.2 %copy-start.26 = (f32[384]{0:T(512)}, f32[384]{0:T(512)S(1)}, u32[]{:S(2)}) copy-start(f32[384]{0:T(512)S(1)} %compare_convert_fusion) | copy-start | bytes 4612
  342.6 356.0 %reduce-scatter.17.cloned.1.call-start = ((), (), s32[]{:S(2)}) async-start(), calls=%async_computation.19 | async-start | bytes 9437184 | tf_op jit(solution)/shard_map/reduce_scatter | solution.py:304
  353.0 346.1 %reduce-scatter.21.cloned.1.call-start = ((), (), s32[]{:S(2)}) async-start(), calls=%async_computation.21 | async-start | bytes 9437184 | tf_op jit(solution)/shard_map/reduce_scatter | solution.py:310
  358.1 11.5 %collective-permute-start = (bf16[384,256]{1,0:T(8,128)(2,1)}, bf16[384,256]{1,0:T(8,128)(2,1)S(1)}, u32[]{:S(2)}, u32[]{:S(2)}) collective-permute-start(bf16[384,256]{1,0:T(8,128)(2,1)} %get-tuple-element.238), channel_id=1, source_target_pairs={{0,1},{1,0},{2,3},{3,2},{4,5},{5,4},{6,7},{7,6},{8,9},{9,8},{10,11... | collective-permute-start | bytes 589832 | tf_op jit(solution)/shard_map/ppermute | solution.py:33
  360.1 17.3 %collective-permute-start.1 = (bf16[384,256]{1,0:T(8,128)(2,1)}, bf16[384,256]{1,0:T(8,128)(2,1)S(1)}, u32[]{:S(2)}, u32[]{:S(2)}) collective-permute-start(bf16[384,256]{1,0:T(8,128)(2,1)} %get-tuple-element.237), channel_id=1, source_target_pairs={{0,2},{1,3},{2,0},{3,1},{4,6},{5,7},{6,4},{7,5},{8,10},{9,11},{10,... | collective-permute-start | bytes 589832 | tf_op jit(solution)/shard_map/ppermute | solution.py:33
  362.4 18.0 %collective-permute-start.2 = (bf16[384,256]{1,0:T(8,128)(2,1)}, bf16[384,256]{1,0:T(8,128)(2,1)S(1)}, u32[]{:S(2)}, u32[]{:S(2)}) collective-permute-start(bf16[384,256]{1,0:T(8,128)(2,1)} %get-tuple-element.236), channel_id=1, source_target_pairs={{0,3},{1,2},{2,1},{3,0},{4,7},{5,6},{6,5},{7,4},{8,11},{9,10},{10,... | collective-permute-start | bytes 589832 | tf_op jit(solution)/shard_map/ppermute | solution.py:33
  610.0 77.6 %all-to-all-start.2 = ((bf16[1536,3,256]{2,1,0:T(4,128)(2,1)}), bf16[1536,3,256]{2,1,0:T(4,128)(2,1)S(1)}, u32[]{:S(2)}, u32[]{:S(2)}) async-start(bf16[1536,3,256]{2,1,0:T(4,128)(2,1)} %copy.89), calls=%async_computation.2 | async-start | bytes 6291456 | tf_op jit(solution)/shard_map/all_to_all | solution.py:264
  614.2 106.4 %reduce-scatter.15.cloned.1.call-start = ((), (), s32[]{:S(2)}) async-start(), calls=%async_computation.18 | async-start | bytes 327680 | tf_op jit(solution)/shard_map/reduce_scatter | solution.py:333
  614.9 143.0 %reduce-scatter.9.cloned.1.call-start = ((), (), s32[]{:S(2)}) async-start(), calls=%async_computation.15 | async-start | bytes 7077888 | tf_op jit(solution)/shard_map/reduce_scatter | solution.py:283
  698.5 106.6 %reduce-scatter.19.cloned.1.call-start = ((), (), s32[]{:S(2)}) async-start(), calls=%async_computation.20 | async-start | bytes 1310720 | tf_op jit(solution)/shard_map/reduce_scatter | solution.py:345
  699.1 116.4 %reduce-scatter.23.cloned.1.call-start = ((), (), s32[]{:S(2)}) async-start(), calls=%async_computation.22 | async-start | bytes 1310720 | tf_op jit(solution)/shard_map/reduce_scatter | solution.py:351
  699.8 139.8 %reduce-scatter.11.cloned.1.call-start = ((), (), s32[]{:S(2)}) async-start(), calls=%async_computation.16 | async-start | bytes 983040 | tf_op jit(solution)/shard_map/reduce_scatter | solution.py:324
  729.5 32.3 %copy-start.34 = (bf16[1024]{0:T(1024)(128)(2,1)S(1)}, bf16[1024]{0:T(1024)(128)(2,1)}, u32[]{:S(2)}) copy-start(bf16[1024]{0:T(1024)(128)(2,1)} %get-tuple-element.222) | copy-start | bytes 6148
  729.5 32.3 %copy-start.35 = (bf16[1024]{0:T(1024)(128)(2,1)S(1)}, bf16[1024]{0:T(1024)(128)(2,1)}, u32[]{:S(2)}) copy-start(bf16[1024]{0:T(1024)(128)(2,1)} %get-tuple-element.235) | copy-start | bytes 6148
  729.5 32.3 %copy-start.36 = (bf16[4096]{0:T(1024)(128)(2,1)S(1)}, bf16[4096]{0:T(1024)(128)(2,1)}, u32[]{:S(2)}) copy-start(bf16[4096]{0:T(1024)(128)(2,1)} %get-tuple-element.245) | copy-start | bytes 24580
  729.5 32.3 %copy-start.41 = (bf16[1024]{0:T(1024)(128)(2,1)S(1)}, bf16[1024]{0:T(1024)(128)(2,1)}, u32[]{:S(2)}) copy-start(bf16[1024]{0:T(1024)(128)(2,1)} %get-tuple-element.153) | copy-start | bytes 6148
  729.5 32.3 %copy-start.42 = (bf16[1024]{0:T(1024)(128)(2,1)S(1)}, bf16[1024]{0:T(1024)(128)(2,1)}, u32[]{:S(2)}) copy-start(bf16[1024]{0:T(1024)(128)(2,1)} %get-tuple-element.159) | copy-start | bytes 6148
  729.5 72.2 %copy-start.10 = (f32[384,1024]{1,0:T(8,128)S(1)}, f32[384,1024]{1,0:T(8,128)}, u32[]{:S(2)}) copy-start(f32[384,1024]{1,0:T(8,128)} %copy-done.9) | copy-start | bytes 4718596
  729.5 72.2 %copy-start.17 = (bf16[384,1024]{1,0:T(8,128)(2,1)S(1)}, bf16[384,1024]{1,0:T(8,128)(2,1)}, u32[]{:S(2)}) copy-start(bf16[384,1024]{1,0:T(8,128)(2,1)} %param.35) | copy-start | bytes 2359300
  729.5 72.2 %copy-start.29 = (f32[384]{0:T(512)S(1)}, f32[384]{0:T(512)}, u32[]{:S(2)}) copy-start(f32[384]{0:T(512)} %copy-done.28) | copy-start | bytes 4612
  (48 other events, 448.2 us)
Sparse Core Ops, SparseCore 0:
  9.9 48.2 all-gather.14
  60.1 27.8 all-gather.16
  89.9 54.3 all-gather.18
  146.1 54.3 all-gather.20
  342.7 41.5 reduce-scatter.12
  388.0 71.2 reduce-scatter.16
  462.8 71.2 reduce-scatter.20
  617.3 25.4 reduce-scatter.14
  698.6 59.2 reduce-scatter.8
  760.1 27.1 reduce-scatter.18
  789.6 25.8 reduce-scatter.22
  817.8 21.8 reduce-scatter.10
